TPU v7x, 32 devices: a whole 2x2x4 slice. The times are simulated.
32 devices in a mesh: slab: 8 (over y, x, core), coil: 4 (over z).
Axes of the slice: x: 2, y: 2, z: 4, core: 2. Of those that a mesh axis runs over, the one named last changes fastest.
Arguments:
- sensitivity: float32 [4, 2, 16, 256, 128], P('coil', None, 'slab'), may hold values from -4 to 4
- kspace: float32 [4, 2, 16, 256, 128], P('coil', None, 'slab')
- sampling: int32 [16, 256, 128], P('slab'), may hold values 0 or 1
- prior_image: float32 [2, 16, 256, 128], P(None, 'slab', 'coil')
- w_first: bfloat16 [32, 2, 3, 3, 3], replicated, may hold values from -0.875 to 0.875
- w_middle: bfloat16 [3, 32, 32, 3, 3, 3], replicated, may hold values from -0.21875 to 0.21875
- w_last: bfloat16 [2, 32, 3, 3, 3], replicated, may hold values from -0.21875 to 0.21875
Outputs:
- solution: float32 [2, 16, 256, 128], P(None, 'slab', 'coil')
- refined: float32 [2, 16, 256, 128], P(None, 'slab', 'coil')
Inputs may be any that keep to these rules, and one draw needn't show every extreme that they name: sampling marks the measured ky-kz positions of each readout plane.
All inputs are finite; a program needn't handle non-finite values. No bound on the sum of `sampling` on one device may be relied on, other than what follows from the above.
Results may differ from a plain program's by a relative error of at most 0.0015.
Values may be sent and summed in bfloat16 or wider, within the bound.
A program may use at most 128 MiB of HBM per device.

v0:
```python
import math
import jax
import jax.numpy as jnp
from jax import lax
from jax.sharding import PartitionSpec as P

ITERS = 2
LAMBDA = 0.5
HIGHEST = lax.Precision.HIGHEST


def extended(cells, sides, width):
    for axis, dim in sides:
        count = lax.axis_size(axis)
        ends = count - 1
        head = lax.slice_in_dim(cells, 0, width, axis=dim)
        tail = lax.slice_in_dim(cells, cells.shape[dim] - width, cells.shape[dim], axis=dim)
        cells = jnp.concatenate(
            [
                lax.ppermute(tail, axis, [(i, (i + 1) % count) for i in range(ends)]),
                cells,
                lax.ppermute(head, axis, [((i + 1) % count, i) for i in range(ends)]),
            ],
            axis=dim,
        )
    return cells


def dft_tables(length, sign):
    positions = jnp.arange(length, dtype=jnp.int32)
    phases = positions[:, None] * positions[None, :] % length
    angles = 2.0 * math.pi / length * phases.astype(jnp.float32)
    scaling = 1.0 / math.sqrt(length)
    return (jnp.cos(angles) * scaling, sign * scaling * jnp.sin(angles))


def transform(field, tables):
    cosine_y, sine_y, cosine_z, sine_z = tables
    plain = jnp.einsum("ky,acpyz->acpkz", cosine_y, field, precision=HIGHEST)
    turned = jnp.einsum("ky,acpyz->acpkz", sine_y, field, precision=HIGHEST)
    field = jnp.stack([plain[0] - turned[1], plain[1] + turned[0]])
    plain = jnp.einsum("acpyz,zk->acpyk", field, cosine_z, precision=HIGHEST)
    turned = jnp.einsum("acpyz,zk->acpyk", field, sine_z, precision=HIGHEST)
    return jnp.stack([plain[0] - turned[1], plain[1] + turned[0]])


def combine_coils(field, coil_maps):
    real_part = jnp.sum(coil_maps[0] * field[0] + coil_maps[1] * field[1], axis=0)
    imag_part = jnp.sum(coil_maps[0] * field[1] - coil_maps[1] * field[0], axis=0)
    return jnp.stack([real_part, imag_part])


def coil_terms(image, coil_maps, mask_f, forward, backward):
    image_re = image[0][None]
    image_im = image[1][None]
    coil_field = jnp.stack(
        [
            coil_maps[0] * image_re - coil_maps[1] * image_im,
            coil_maps[0] * image_im + coil_maps[1] * image_re,
        ]
    )
    spectrum = transform(coil_field, forward) * mask_f
    energy = jnp.sum(spectrum * spectrum)
    return (combine_coils(transform(spectrum, backward), coil_maps), energy)


def coil_total(local_image):
    return lax.psum(local_image, "coil")


def image_total(value):
    return lax.psum(value, "slab")


def curvature(direction, energy):
    weight_share = LAMBDA / lax.axis_size("coil")
    local_sum = energy + weight_share * jnp.sum(direction * direction)
    return lax.psum(local_sum, ("slab", "coil"))


def shift_right(values):
    zero_column = jnp.zeros(values.shape[:-1] + (1,), values.dtype)
    return jnp.concatenate([zero_column, values[..., :-1]], axis=-1)


def shift_left(values):
    zero_column = jnp.zeros(values.shape[:-1] + (1,), values.dtype)
    return jnp.concatenate([values[..., 1:], zero_column], axis=-1)


def conv_layer(activation, weight):
    padded = extended(activation, (("slab", 1), ("coil", 2)), 1)
    plane_count = activation.shape[1]
    row_count = activation.shape[2]
    out_channels = weight.shape[0]
    totals = [
        jnp.zeros((out_channels,) + activation.shape[1:], jnp.float32) for offset_z in range(3)
    ]
    for shift_x in range(3):
        for shift_y in range(3):
            window = padded[:, shift_x : shift_x + plane_count, shift_y : shift_y + row_count, :]
            tap_weights = weight[:, :, shift_x, shift_y, :]
            stacked = jnp.einsum(
                "oit,ipyz->topyz", tap_weights, window, preferred_element_type=jnp.float32
            )
            for offset_z in range(3):
                totals[offset_z] = totals[offset_z] + stacked[offset_z]
    return totals[1] + shift_right(totals[0]) + shift_left(totals[2])


def body(sensitivity, kspace, sampling, prior_image, w_first, w_middle, w_last):
    coil_maps = jnp.moveaxis(sensitivity, 1, 0)
    measured = jnp.moveaxis(kspace, 1, 0)
    mask_f = sampling.astype(jnp.float32)
    len_y = coil_maps.shape[3]
    len_z = coil_maps.shape[4]
    forward = dft_tables(len_y, -1.0) + dft_tables(len_z, -1.0)
    backward = dft_tables(len_y, 1.0) + dft_tables(len_z, 1.0)
    block_rows = prior_image.shape[2]
    prior_view = lax.all_gather(prior_image, "coil", axis=2, tiled=True)
    adjoint_local = combine_coils(transform(measured * mask_f, backward), coil_maps)
    rhs = coil_total(adjoint_local) + LAMBDA * prior_view
    solution = jnp.zeros_like(rhs)
    residual = rhs
    direction = rhs
    norm_now = image_total(jnp.sum(residual * residual))
    for step_index in range(ITERS):
        local_q, energy = coil_terms(direction, coil_maps, mask_f, forward, backward)
        image_q = coil_total(local_q) + LAMBDA * direction
        step_size = norm_now / curvature(direction, energy)
        solution = solution + step_size * direction
        if step_index + 1 < ITERS:
            residual = residual - step_size * image_q
            norm_next = image_total(jnp.sum(residual * residual))
            direction = residual + norm_next / norm_now * direction
            norm_now = norm_next
    brick = lax.dynamic_slice_in_dim(solution, lax.axis_index("coil") * block_rows, block_rows, 2)
    features = brick.astype(jnp.bfloat16)
    hidden = jax.nn.relu(conv_layer(features, w_first)).astype(jnp.bfloat16)
    for layer_index in range(w_middle.shape[0]):
        hidden = jax.nn.relu(conv_layer(hidden, w_middle[layer_index])).astype(jnp.bfloat16)
    correction = conv_layer(hidden, w_last)
    return (brick, brick + correction)


def solution(mesh):
    placed = (
        P("coil", None, "slab", None, None),
        P("coil", None, "slab", None, None),
        P("slab", None, None),
        P(None, "slab", "coil", None),
        P(),
        P(),
        P(),
    )
    return jax.shard_map(
        body,
        mesh=mesh,
        in_specs=placed,
        out_specs=(P(None, "slab", "coil", None), P(None, "slab", "coil", None)),
        check_vma=False,
    )
```

profile of v0, /device:TPU:6, one launch (start us, length us, event | category | flops | bytes accessed | tf_op | source)
XLA Modules:
  0.0 498.4 jit_solution(12519650154397475423)
XLA Ops:
  17.3 22.0 %all_gather.3 = f32[2,2,256,128]{3,2,1,0:T(8,128)S(1)} all-gather(f32[2,2,64,128]{3,2,1,0:T(8,128)S(1)} %copy-done.6), channel_id=1, replica_groups=mesh['slab'=8,'coil'=4] {'coil'}, dimensions={2}, use_global_device_ids=true | all-gather | bytes 655360 | tf_op jit(solution)/shard_map/all_gather | solution.py:120
  39.3 21.7 %all-reduce.13.cloned.1.call-done = f32[2,2,256,128]{3,2,1,0:T(8,128)} async-done(((f32[2,2,256,128]{3,2,1,0:T(8,128)}), f32[2,2,256,128]{3,2,1,0:T(8,128)}) %all-reduce.13.cloned.1.call-update) | async-done | bytes 524304 | tf_op jit(solution)/shard_map/psum | solution.py:68
  78.4 40.5 %psum.44 = f32[]{:T(128)} all-reduce(f32[]{:T(128)S(6)} %add.651), channel_id=1, replica_groups=mesh['slab'=8,'coil'=4] {'slab','coil'}, use_global_device_ids=true, to_apply=%region_4.5 | all-reduce | flops 1 | bytes 8 | tf_op jit(solution)/shard_map/psum | solution.py:78
  118.9 10.9 %psum.43 = f32[]{:T(128)} all-reduce(f32[]{:T(128)} %get-tuple-element.6), channel_id=1, replica_groups=mesh['slab'=8,'coil'=4] {'slab'}, use_global_device_ids=true, to_apply=%region_2.3 | all-reduce | flops 1 | bytes 8 | tf_op jit(solution)/shard_map/psum | solution.py:72
  133.0 13.2 %psum.46 = f32[]{:T(128)} all-reduce(f32[]{:T(128)} %multiply_reduce_fusion.1), channel_id=1, replica_groups=mesh['slab'=8,'coil'=4] {'slab'}, use_global_device_ids=true, to_apply=%region_7.8 | all-reduce | flops 1 | bytes 8 | tf_op jit(solution)/shard_map/psum | solution.py:72
  157.5 40.9 %psum.47 = f32[]{:T(128)} all-reduce(f32[]{:T(128)S(6)} %add.660), channel_id=1, replica_groups=mesh['slab'=8,'coil'=4] {'slab','coil'}, use_global_device_ids=true, to_apply=%region_10.11 | all-reduce | flops 1 | bytes 8 | tf_op jit(solution)/shard_map/psum | solution.py:78
  217.8 3.6 convolution_bitcast_fusion.29
  228.7 3.7 convolution_bitcast_fusion.33
  232.3 3.7 convolution_bitcast_fusion.35
  236.1 5.2 %fusion.22 = f32[32,2,64,128]{3,0,2,1:T(8,128)S(1)} fusion(f32[3,32,2,64,128]{4,1,3,2,0:T(8,128)S(1)} %convolution_bitcast_fusion.27, f32[3,32,2,64,128]{4,1,3,2,0:T(8,128)S(1)} %convolution_bitcast_fusion.28, f32[3,32,2,64,128]{4,1,3,2,0:T(8,128)} %convolution_bitcast_fusion.29, f32[3,32,2,64,128]{4,1,3,2,0:T(8,128)} %convolution_bitcast_fusion.30, ...), kind=kLoop, calls=%fused_computation.139 | loop fusion | flops 4194304 | bytes 20971520 | tf_op jit(solution)/shard_map/add | solution.py:107
  241.3 5.2 %fusion.30 = f32[32,2,64,128]{3,0,2,1:T(8,128)S(1)} fusion(f32[3,32,2,64,128]{4,1,3,2,0:T(8,128)S(1)} %convolution_bitcast_fusion.27, f32[3,32,2,64,128]{4,1,3,2,0:T(8,128)S(1)} %convolution_bitcast_fusion.28, f32[3,32,2,64,128]{4,1,3,2,0:T(8,128)} %convolution_bitcast_fusion.29, f32[3,32,2,64,128]{4,1,3,2,0:T(8,128)} %convolution_bitcast_fusion.30, ...), kind=kLoop, calls=%fused_computation.155 | loop fusion | flops 4194304 | bytes 20971520 | tf_op jit(solution)/shard_map/add | solution.py:107
  247.1 5.4 %fusion.35 = bf16[32,2,64,128]{3,0,2,1:T(8,128)(2,1)S(1)} fusion(f32[3,32,2,64,128]{4,1,3,2,0:T(8,128)S(1)} %convolution_bitcast_fusion.27, f32[3,32,2,64,128]{4,1,3,2,0:T(8,128)S(1)} %convolution_bitcast_fusion.28, f32[3,32,2,64,128]{4,1,3,2,0:T(8,128)} %convolution_bitcast_fusion.29, f32[3,32,2,64,128]{4,1,3,2,0:T(8,128)} %convolution_bitcast_fusion.30, ...), kind=kLoop, calls=%fused_computation.169 | loop fusion | flops 6291456 | bytes 24084480 | tf_op jit(solution)/shard_map/convert_element_type | solution.py:139
  261.4 7.6 %collective-permute-done.4 = bf16[32,1,64,128]{3,0,2,1:T(8,128)(2,1)S(1)} collective-permute-done((bf16[32,1,64,128]{3,0,2,1:T(8,128)(2,1)S(1)}, bf16[32,1,64,128]{3,0,2,1:T(8,128)(2,1)S(1)}, u32[]{:S(2)}, u32[]{:S(2)}) %collective-permute-start.4) | collective-permute-done | bytes 524320 | tf_op jit(solution)/shard_map/ppermute | solution.py:20
  274.3 3.7 convolution_bitcast_fusion.25
  293.0 3.7 convolution_bitcast_fusion.24
  300.2 13.8 %fusion.15 = (f32[32,2,64,128]{3,0,2,1:T(8,128)}, f32[32,2,64,128]{3,0,2,1:T(8,128)}) fusion(f32[3,32,2,64,128]{4,1,3,2,0:T(8,128)} %convolution_bitcast_fusion.18, f32[3,32,2,64,128]{4,1,3,2,0:T(8,128)S(1)} %convolution_bitcast_fusion.19, f32[3,32,2,64,128]{4,1,3,2,0:T(8,128)} %convolution_bitcast_fusion.20, ...), kind=kLoop, calls=%fused_computation.116 | loop fusion | flops 8388608 | bytes 41943040 | tf_op jit(solution)/shard_map/add | solution.py:107
  316.4 6.6 %fusion.20 = bf16[32,2,64,128]{3,0,2,1:T(8,128)(2,1)S(1)} fusion(f32[3,32,2,64,128]{4,1,3,2,0:T(8,128)} %convolution_bitcast_fusion.18, f32[3,32,2,64,128]{4,1,3,2,0:T(8,128)S(1)} %convolution_bitcast_fusion.19, f32[3,32,2,64,128]{4,1,3,2,0:T(8,128)} %convolution_bitcast_fusion.20, f32[3,32,2,64,128]{4,1,3,2,0:T(8,128)} %convolution_bitcast_fusion.21, ...), kind=kLoop, calls=%fused_computation.129 | loop fusion | flops 6291456 | bytes 24084480 | tf_op jit(solution)/shard_map/convert_element_type | solution.py:141
  331.7 6.4 %collective-permute-done.8 = bf16[32,1,64,128]{3,0,2,1:T(8,128)(2,1)S(1)} collective-permute-done((bf16[32,1,64,128]{3,0,2,1:T(8,128)(2,1)S(1)}, bf16[32,1,64,128]{3,0,2,1:T(8,128)(2,1)S(1)}, u32[]{:S(2)}, u32[]{:S(2)}) %collective-permute-start.8) | collective-permute-done | bytes 524320 | tf_op jit(solution)/shard_map/ppermute | solution.py:20
  338.1 4.5 collective-permute-start.10
  344.9 3.7 convolution_bitcast_fusion.16
  363.6 3.7 convolution_bitcast_fusion.15
  370.9 13.8 %fusion.8 = (f32[32,2,64,128]{3,0,2,1:T(8,128)}, f32[32,2,64,128]{3,0,2,1:T(8,128)}) fusion(f32[3,32,2,64,128]{4,1,3,2,0:T(8,128)} %convolution_bitcast_fusion.9, f32[3,32,2,64,128]{4,1,3,2,0:T(8,128)S(1)} %convolution_bitcast_fusion.10, f32[3,32,2,64,128]{4,1,3,2,0:T(8,128)} %convolution_bitcast_fusion.11, ...), kind=kLoop, calls=%fused_computation.85 | loop fusion | flops 8388608 | bytes 41943040 | tf_op jit(solution)/shard_map/add | solution.py:107
  387.1 6.6 %fusion.13 = bf16[32,2,64,128]{3,0,2,1:T(8,128)(2,1)S(1)} fusion(f32[3,32,2,64,128]{4,1,3,2,0:T(8,128)} %convolution_bitcast_fusion.9, f32[3,32,2,64,128]{4,1,3,2,0:T(8,128)S(1)} %convolution_bitcast_fusion.10, f32[3,32,2,64,128]{4,1,3,2,0:T(8,128)} %convolution_bitcast_fusion.11, f32[3,32,2,64,128]{4,1,3,2,0:T(8,128)} %convolution_bitcast_fusion.12, ...), kind=kLoop, calls=%fused_computation.98 | loop fusion | flops 6291456 | bytes 24084480 | tf_op jit(solution)/shard_map/convert_element_type | solution.py:141
  402.3 5.1 %collective-permute-done.12 = bf16[32,1,64,128]{3,0,2,1:T(8,128)(2,1)S(1)} collective-permute-done((bf16[32,1,64,128]{3,0,2,1:T(8,128)(2,1)S(1)}, bf16[32,1,64,128]{3,0,2,1:T(8,128)(2,1)S(1)}, u32[]{:S(2)}, u32[]{:S(2)}) %collective-permute-start.12) | collective-permute-done | bytes 524320 | tf_op jit(solution)/shard_map/ppermute | solution.py:20
  407.5 4.3 collective-permute-start.14
  414.0 3.7 convolution_bitcast_fusion.7
  432.7 3.7 convolution_bitcast_fusion.6
  439.9 13.8 %fusion.1 = (f32[32,2,64,128]{3,0,2,1:T(8,128)}, f32[32,2,64,128]{3,0,2,1:T(8,128)}) fusion(f32[3,32,2,64,128]{4,1,3,2,0:T(8,128)} %convolution_bitcast_fusion, f32[3,32,2,64,128]{4,1,3,2,0:T(8,128)S(1)} %convolution_bitcast_fusion.1, f32[3,32,2,64,128]{4,1,3,2,0:T(8,128)} %convolution_bitcast_fusion.2, f32[3,32,2,64,128]{4,1,3,2,0:T(8,128)} %convolution_bitcast_fusion.3, ...), kind=kLoop, calls=%fused_computation.54 | loop fusion | flops 8388608 | bytes 41943040 | tf_op jit(solution)/shard_map/add | solution.py:107
  456.1 6.6 %fusion.6 = bf16[32,2,64,128]{3,0,2,1:T(8,128)(2,1)S(1)} fusion(f32[3,32,2,64,128]{4,1,3,2,0:T(8,128)} %convolution_bitcast_fusion, f32[3,32,2,64,128]{4,1,3,2,0:T(8,128)S(1)} %convolution_bitcast_fusion.1, f32[3,32,2,64,128]{4,1,3,2,0:T(8,128)} %convolution_bitcast_fusion.2, f32[3,32,2,64,128]{4,1,3,2,0:T(8,128)} %convolution_bitcast_fusion.3, ...), kind=kLoop, calls=%fused_computation.67 | loop fusion | flops 6291456 | bytes 24084480 | tf_op jit(solution)/shard_map/convert_element_type | solution.py:141
  467.6 3.8 collective-permute-done.17
  471.4 4.7 collective-permute-done.16
  476.2 4.6 collective-permute-start.18
  (161 shorter events, 175.9 us)
Async XLA Ops:
  7.2 53.9 %all-reduce.13.cloned.1.call-start = ((), (), s32[]{:S(2)}) async-start(), calls=%async_computation | async-start | bytes 1048576 | tf_op jit(solution)/shard_map/psum | solution.py:68
  13.9 2.4 copy-start.3
  16.3 1.0 copy-start.6
  17.3 113.9 %all-reduce.15.cloned.1.call-start = ((), (), s32[]{:S(2)}) async-start(), calls=%async_computation.1 | async-start | bytes 1048576 | tf_op jit(solution)/shard_map/psum | solution.py:68
  154.3 50.5 %copy-start.7 = (bf16[32,2,3,3,3]{0,1,4,3,2:T(2,128)(2,1)S(1)}, bf16[32,2,3,3,3]{0,1,4,3,2:T(2,128)(2,1)}, u32[]{:S(2)}) copy-start(bf16[32,2,3,3,3]{0,1,4,3,2:T(2,128)(2,1)} %param.11) | copy-start | bytes 10372
  200.5 5.4 %collective-permute-start.1 = (bf16[2,1,64,128]{3,2,1,0:T(8,128)(2,1)S(1)}, bf16[2,1,64,128]{3,2,1,0:T(8,128)(2,1)S(1)}, u32[]{:S(2)}, u32[]{:S(2)}) collective-permute-start(bf16[2,1,64,128]{3,2,1,0:T(8,128)(2,1)S(1)} %get-tuple-element.76), channel_id=1, source_target_pairs={{4,0},{8,4},{12,8},{16,12},{20,16},{24,20},{28,24},{5,1},{9,5},{13... | collective-permute-start | bytes 98312 | tf_op jit(solution)/shard_map/ppermute | solution.py:22
  202.4 5.2 %collective-permute-start = (bf16[2,1,64,128]{3,2,1,0:T(8,128)(2,1)S(1)}, bf16[2,1,64,128]{3,2,1,0:T(8,128)(2,1)S(1)}, u32[]{:S(2)}, u32[]{:S(2)}) collective-permute-start(bf16[2,1,64,128]{3,2,1,0:T(8,128)(2,1)S(1)} %get-tuple-element.75), channel_id=1, source_target_pairs={{0,4},{4,8},{8,12},{12,16},{16,20},{20,24},{24,28},{1,5},{5,9},{9,... | collective-permute-start | bytes 98312 | tf_op jit(solution)/shard_map/ppermute | solution.py:20
  207.7 7.0 %collective-permute-start.2 = (bf16[2,4,1,128]{3,2,1,0:T(2,128)(2,1)S(1)}, bf16[2,4,1,128]{3,2,1,0:T(2,128)(2,1)S(1)}, u32[]{:S(2)}, u32[]{:S(2)}) collective-permute-start(bf16[2,4,1,128]{3,2,1,0:T(2,128)(2,1)S(1)} %get-tuple-element.71), channel_id=1, source_target_pairs={{0,1},{1,2},{2,3},{4,5},{5,6},{6,7},{8,9},{9,10},{10,11},{12,13},{... | collective-permute-start | bytes 6152 | tf_op jit(solution)/shard_map/ppermute | solution.py:20
  211.1 5.5 %collective-permute-start.3 = (bf16[2,4,1,128]{3,2,1,0:T(2,128)(2,1)S(1)}, bf16[2,4,1,128]{3,2,1,0:T(2,128)(2,1)S(1)}, u32[]{:S(2)}, u32[]{:S(2)}) collective-permute-start(bf16[2,4,1,128]{3,2,1,0:T(2,128)(2,1)S(1)} %get-tuple-element.72), channel_id=1, source_target_pairs={{1,0},{2,1},{3,2},{5,4},{6,5},{7,6},{9,8},{10,9},{11,10},{13,12},{... | collective-permute-start | bytes 6152 | tf_op jit(solution)/shard_map/ppermute | solution.py:22
  252.5 4.6 copy-start.4
  252.6 8.7 %collective-permute-start.5 = (bf16[32,1,64,128]{3,0,2,1:T(8,128)(2,1)S(1)}, bf16[32,1,64,128]{3,0,2,1:T(8,128)(2,1)S(1)}, u32[]{:S(2)}, u32[]{:S(2)}) collective-permute-start(bf16[32,1,64,128]{3,0,2,1:T(8,128)(2,1)S(1)} %get-tuple-element.43), channel_id=1, source_target_pairs={{4,0},{8,4},{12,8},{16,12},{20,16},{24,20},{28,24},{5,1},{9,5},{13... | collective-permute-start | bytes 1572872 | tf_op jit(solution)/shard_map/ppermute | solution.py:22
  254.7 14.3 %collective-permute-start.4 = (bf16[32,1,64,128]{3,0,2,1:T(8,128)(2,1)S(1)}, bf16[32,1,64,128]{3,0,2,1:T(8,128)(2,1)S(1)}, u32[]{:S(2)}, u32[]{:S(2)}) collective-permute-start(bf16[32,1,64,128]{3,0,2,1:T(8,128)(2,1)S(1)} %get-tuple-element.42), channel_id=1, source_target_pairs={{0,4},{4,8},{8,12},{12,16},{16,20},{20,24},{24,28},{1,5},{5,9},{9,... | collective-permute-start | bytes 1572872 | tf_op jit(solution)/shard_map/ppermute | solution.py:20
  269.0 8.9 %collective-permute-start.6 = (bf16[32,4,1,128]{3,0,2,1:T(8,128)(2,1)S(1)}, bf16[32,4,1,128]{3,0,2,1:T(8,128)(2,1)S(1)}, u32[]{:S(2)}, u32[]{:S(2)}) collective-permute-start(bf16[32,4,1,128]{3,0,2,1:T(8,128)(2,1)S(1)} %get-tuple-element.30), channel_id=1, source_target_pairs={{0,1},{1,2},{2,3},{4,5},{5,6},{6,7},{8,9},{9,10},{10,11},{12,13},{... | collective-permute-start | bytes 98312 | tf_op jit(solution)/shard_map/ppermute | solution.py:20
  272.0 5.9 %collective-permute-start.7 = (bf16[32,4,1,128]{3,0,2,1:T(8,128)(2,1)S(1)}, bf16[32,4,1,128]{3,0,2,1:T(8,128)(2,1)S(1)}, u32[]{:S(2)}, u32[]{:S(2)}) collective-permute-start(bf16[32,4,1,128]{3,0,2,1:T(8,128)(2,1)S(1)} %get-tuple-element.31), channel_id=1, source_target_pairs={{1,0},{2,1},{3,2},{5,4},{6,5},{7,6},{9,8},{10,9},{11,10},{13,12},{... | collective-permute-start | bytes 98312 | tf_op jit(solution)/shard_map/ppermute | solution.py:22
  314.0 2.4 copy-start
  323.1 8.6 %collective-permute-start.9 = (bf16[32,1,64,128]{3,0,2,1:T(8,128)(2,1)S(1)}, bf16[32,1,64,128]{3,0,2,1:T(8,128)(2,1)S(1)}, u32[]{:S(2)}, u32[]{:S(2)}) collective-permute-start(bf16[32,1,64,128]{3,0,2,1:T(8,128)(2,1)S(1)} %get-tuple-element.41), channel_id=1, source_target_pairs={{4,0},{8,4},{12,8},{16,12},{20,16},{24,20},{28,24},{5,1},{9,5},{13... | collective-permute-start | bytes 1572872 | tf_op jit(solution)/shard_map/ppermute | solution.py:22
  325.0 13.1 %collective-permute-start.8 = (bf16[32,1,64,128]{3,0,2,1:T(8,128)(2,1)S(1)}, bf16[32,1,64,128]{3,0,2,1:T(8,128)(2,1)S(1)}, u32[]{:S(2)}, u32[]{:S(2)}) collective-permute-start(bf16[32,1,64,128]{3,0,2,1:T(8,128)(2,1)S(1)} %get-tuple-element.40), channel_id=1, source_target_pairs={{0,4},{4,8},{8,12},{12,16},{16,20},{20,24},{24,28},{1,5},{5,9},{9,... | collective-permute-start | bytes 1572872 | tf_op jit(solution)/shard_map/ppermute | solution.py:20
  338.1 10.5 %collective-permute-start.10 = (bf16[32,4,1,128]{3,0,2,1:T(8,128)(2,1)S(1)}, bf16[32,4,1,128]{3,0,2,1:T(8,128)(2,1)S(1)}, u32[]{:S(2)}, u32[]{:S(2)}) collective-permute-start(bf16[32,4,1,128]{3,0,2,1:T(8,128)(2,1)S(1)} %get-tuple-element.26), channel_id=1, source_target_pairs={{0,1},{1,2},{2,3},{4,5},{5,6},{6,7},{8,9},{9,10},{10,11},{12,13},{... | collective-permute-start | bytes 98312 | tf_op jit(solution)/shard_map/ppermute | solution.py:20
  342.7 5.9 %collective-permute-start.11 = (bf16[32,4,1,128]{3,0,2,1:T(8,128)(2,1)S(1)}, bf16[32,4,1,128]{3,0,2,1:T(8,128)(2,1)S(1)}, u32[]{:S(2)}, u32[]{:S(2)}) collective-permute-start(bf16[32,4,1,128]{3,0,2,1:T(8,128)(2,1)S(1)} %get-tuple-element.27), channel_id=1, source_target_pairs={{1,0},{2,1},{3,2},{5,4},{6,5},{7,6},{9,8},{10,9},{11,10},{13,12},{... | collective-permute-start | bytes 98312 | tf_op jit(solution)/shard_map/ppermute | solution.py:22
  384.7 2.4 copy-start.1
  393.7 8.6 %collective-permute-start.13 = (bf16[32,1,64,128]{3,0,2,1:T(8,128)(2,1)S(1)}, bf16[32,1,64,128]{3,0,2,1:T(8,128)(2,1)S(1)}, u32[]{:S(2)}, u32[]{:S(2)}) collective-permute-start(bf16[32,1,64,128]{3,0,2,1:T(8,128)(2,1)S(1)} %get-tuple-element.39), channel_id=1, source_target_pairs={{4,0},{8,4},{12,8},{16,12},{20,16},{24,20},{28,24},{5,1},{9,5},{13... | collective-permute-start | bytes 1572872 | tf_op jit(solution)/shard_map/ppermute | solution.py:22
  395.7 11.8 %collective-permute-start.12 = (bf16[32,1,64,128]{3,0,2,1:T(8,128)(2,1)S(1)}, bf16[32,1,64,128]{3,0,2,1:T(8,128)(2,1)S(1)}, u32[]{:S(2)}, u32[]{:S(2)}) collective-permute-start(bf16[32,1,64,128]{3,0,2,1:T(8,128)(2,1)S(1)} %get-tuple-element.38), channel_id=1, source_target_pairs={{0,4},{4,8},{8,12},{12,16},{16,20},{20,24},{24,28},{1,5},{5,9},{9,... | collective-permute-start | bytes 1572872 | tf_op jit(solution)/shard_map/ppermute | solution.py:20
  407.5 10.2 %collective-permute-start.14 = (bf16[32,4,1,128]{3,0,2,1:T(8,128)(2,1)S(1)}, bf16[32,4,1,128]{3,0,2,1:T(8,128)(2,1)S(1)}, u32[]{:S(2)}, u32[]{:S(2)}) collective-permute-start(bf16[32,4,1,128]{3,0,2,1:T(8,128)(2,1)S(1)} %get-tuple-element.22), channel_id=1, source_target_pairs={{0,1},{1,2},{2,3},{4,5},{5,6},{6,7},{8,9},{9,10},{10,11},{12,13},{... | collective-permute-start | bytes 98312 | tf_op jit(solution)/shard_map/ppermute | solution.py:20
  411.7 5.9 %collective-permute-start.15 = (bf16[32,4,1,128]{3,0,2,1:T(8,128)(2,1)S(1)}, bf16[32,4,1,128]{3,0,2,1:T(8,128)(2,1)S(1)}, u32[]{:S(2)}, u32[]{:S(2)}) collective-permute-start(bf16[32,4,1,128]{3,0,2,1:T(8,128)(2,1)S(1)} %get-tuple-element.23), channel_id=1, source_target_pairs={{1,0},{2,1},{3,2},{5,4},{6,5},{7,6},{9,8},{10,9},{11,10},{13,12},{... | collective-permute-start | bytes 98312 | tf_op jit(solution)/shard_map/ppermute | solution.py:22
  453.8 2.4 copy-start.2
  462.7 4.5 copy-start.8
  462.8 8.6 %collective-permute-start.17 = (bf16[32,1,64,128]{3,0,2,1:T(8,128)(2,1)S(1)}, bf16[32,1,64,128]{3,0,2,1:T(8,128)(2,1)S(1)}, u32[]{:S(2)}, u32[]{:S(2)}) collective-permute-start(bf16[32,1,64,128]{3,0,2,1:T(8,128)(2,1)S(1)} %get-tuple-element.37), channel_id=1, source_target_pairs={{4,0},{8,4},{12,8},{16,12},{20,16},{24,20},{28,24},{5,1},{9,5},{13... | collective-permute-start | bytes 1572872 | tf_op jit(solution)/shard_map/ppermute | solution.py:22
  464.8 11.4 %collective-permute-start.16 = (bf16[32,1,64,128]{3,0,2,1:T(8,128)(2,1)S(1)}, bf16[32,1,64,128]{3,0,2,1:T(8,128)(2,1)S(1)}, u32[]{:S(2)}, u32[]{:S(2)}) collective-permute-start(bf16[32,1,64,128]{3,0,2,1:T(8,128)(2,1)S(1)} %get-tuple-element.36), channel_id=1, source_target_pairs={{0,4},{4,8},{8,12},{12,16},{16,20},{20,24},{24,28},{1,5},{5,9},{9,... | collective-permute-start | bytes 1572872 | tf_op jit(solution)/shard_map/ppermute | solution.py:20
  476.2 6.9 %collective-permute-start.18 = (bf16[32,4,1,128]{3,0,2,1:T(8,128)(2,1)S(1)}, bf16[32,4,1,128]{3,0,2,1:T(8,128)(2,1)S(1)}, u32[]{:S(2)}, u32[]{:S(2)}) collective-permute-start(bf16[32,4,1,128]{3,0,2,1:T(8,128)(2,1)S(1)} %get-tuple-element.18), channel_id=1, source_target_pairs={{0,1},{1,2},{2,3},{4,5},{5,6},{6,7},{8,9},{9,10},{10,11},{12,13},{... | collective-permute-start | bytes 98312 | tf_op jit(solution)/shard_map/ppermute | solution.py:20
  480.7 5.8 %collective-permute-start.19 = (bf16[32,4,1,128]{3,0,2,1:T(8,128)(2,1)S(1)}, bf16[32,4,1,128]{3,0,2,1:T(8,128)(2,1)S(1)}, u32[]{:S(2)}, u32[]{:S(2)}) collective-permute-start(bf16[32,4,1,128]{3,0,2,1:T(8,128)(2,1)S(1)} %get-tuple-element.19), channel_id=1, source_target_pairs={{1,0},{2,1},{3,2},{5,4},{6,5},{7,6},{9,8},{10,9},{11,10},{13,12},{... | collective-permute-start | bytes 98312 | tf_op jit(solution)/shard_map/ppermute | solution.py:22
  489.4 0.9 copy-start.5
Sparse Core Ops, SparseCore 0:
  17.4 43.5 all-reduce.12
  76.5 38.5 all-reduce.14
where the time goes:
time: 505 us; the launch traced here: 498 us
  matrix products  132 us (26%)
  blocking collectives  128 us (25%)
  other arithmetic  91.8 us (18%)
  waiting for transfers between devices  66.1 us (13%)
  starting transfers between devices  49.1 us (10%)
  between operations  22 us (4%)
  local copies, waits for them, and re-layouts  9.42 us (2%)
    dot_general x45, matrix products, conv_layer(): jnp.einsum('oit,ipyz->topyz', tap_weights, window, preferred_element_type...  106 us
    psum x2, blocking collectives, curvature(): return lax.psum(local_sum, ('slab', 'coil'))  81.4 us
    add x6, other arithmetic, conv_layer(): totals[offset_z] = totals[offset_z] + stacked[offset_z]  52.1 us
    ppermute x10, starting transfers between devices, extended(): lax.ppermute(tail, axis, [(i, (i + 1) % count) for i in range(ends)])  32.4 us
    ppermute x10, waiting for transfers between devices, extended(): lax.ppermute(tail, axis, [(i, (i + 1) % count) for i in range(ends)])  25.7 us
    psum x2, blocking collectives, image_total(): return lax.psum(value, 'slab')  24.2 us
    all_gather x1, blocking collectives, body(): prior_view = lax.all_gather(prior_image, 'coil', axis=2, tiled=True)  22 us
    psum x2, waiting for transfers between devices, coil_total(): return lax.psum(local_image, 'coil')  21.7 us
  transfers between devices with their start and end apart: 22, of which 12 were waited for; matrix products, arithmetic and copies ran while one was open for 4% of the time, Pallas kernels for 0%

commit v1 on v0

--- a/solution.py
+++ b/solution.py
@@ -75,7 +75,7 @@
 def curvature(direction, energy):
     weight_share = LAMBDA / lax.axis_size("coil")
     local_sum = energy + weight_share * jnp.sum(direction * direction)
-    return lax.psum(local_sum, ("slab", "coil"))
+    return lax.psum(lax.psum(local_sum, "slab"), "coil")
 
 
 def shift_right(values):

time: 505 us -> 468 us (0.927)
  blocking collectives: 128 us -> 78 us
  waiting for transfers between devices: 66.1 us -> 81.4 us
    psum x2 -> x3, blocking collectives: 81.4 us -> 34.7 us  [curvature(): return lax.psum(lax.psum(local_sum, 'slab'), 'coil')]
    psum x2, waiting for transfers between devices: 21.7 us -> 35.2 us  [coil_total(): return lax.psum(local_image, 'coil')]
  transfers between devices with their start and end apart: 22 -> 22, of which waited for: 12 -> 13; matrix products, arithmetic and copies ran while one was open for 4% -> 5% of each run, Pallas kernels for 0% -> 0%
where the time goes in v1:
time: 468 us; the launch traced here: 462 us
  matrix products  132 us (28%)
  other arithmetic  91.9 us (20%)
  waiting for transfers between devices  81.4 us (17%)
  blocking collectives  78 us (17%)
  starting transfers between devices  47.2 us (10%)
  between operations  22 us (5%)
  local copies, waits for them, and re-layouts  9.42 us (2%)
    dot_general x45, matrix products, conv_layer(): jnp.einsum('oit,ipyz->topyz', tap_weights, window, preferred_element_type...  106 us
    add x6, other arithmetic, conv_layer(): totals[offset_z] = totals[offset_z] + stacked[offset_z]  52.1 us
    psum x2, waiting for transfers between devices, coil_total(): return lax.psum(local_image, 'coil')  35.2 us
    psum x3, blocking collectives, curvature(): return lax.psum(lax.psum(local_sum, 'slab'), 'coil')  34.7 us
    ppermute x10, starting transfers between devices, extended(): lax.ppermute(tail, axis, [(i, (i + 1) % count) for i in range(ends)])  30.5 us
    ppermute x10, waiting for transfers between devices, extended(): lax.ppermute(tail, axis, [(i, (i + 1) % count) for i in range(ends)])  27.5 us
    all_gather x1, blocking collectives, body(): prior_view = lax.all_gather(prior_image, 'coil', axis=2, tiled=True)  22 us
    psum x2, blocking collectives, image_total(): return lax.psum(value, 'slab')  21.3 us
  transfers between devices with their start and end apart: 22, of which 13 were waited for; matrix products, arithmetic and copies ran while one was open for 5% of the time, Pallas kernels for 0%

profile of v1, /device:TPU:6, one launch (start us, length us, event | category | flops | bytes accessed | tf_op | source)
XLA Modules:
  0.0 462.1 jit_solution(16886123190111998481)
XLA Ops:
  17.4 22.0 %all_gather.3 = f32[2,2,256,128]{3,2,1,0:T(8,128)S(1)} all-gather(f32[2,2,64,128]{3,2,1,0:T(8,128)S(1)} %copy-done.6), channel_id=1, replica_groups=mesh['slab'=8,'coil'=4] {'coil'}, dimensions={2}, use_global_device_ids=true | all-gather | bytes 655360 | tf_op jit(solution)/shard_map/all_gather | solution.py:120
  39.4 21.7 %all-reduce.14.cloned.1.call-done = f32[2,2,256,128]{3,2,1,0:T(8,128)} async-done(((f32[2,2,256,128]{3,2,1,0:T(8,128)}), f32[2,2,256,128]{3,2,1,0:T(8,128)}) %all-reduce.14.cloned.1.call-update) | async-done | bytes 524304 | tf_op jit(solution)/shard_map/psum | solution.py:68
  78.4 10.6 %all-reduce.10 = (f32[]{:T(128)}, f32[]{:T(128)}) all-reduce(f32[]{:T(128)} %get-tuple-element.8, f32[]{:T(128)S(6)} %add.655), channel_id=1, replica_groups=mesh['slab'=8,'coil'=4] {'slab'}, use_global_device_ids=true, to_apply=%region_2.3 | all-reduce | flops 2 | bytes 16 | tf_op jit(solution)/shard_map/psum | solution.py:72
  89.0 11.2 %psum.59 = f32[]{:T(128)} all-reduce(f32[]{:T(128)} %get-tuple-element.3), channel_id=1, replica_groups=mesh['slab'=8,'coil'=4] {'coil'}, use_global_device_ids=true, to_apply=%region_5.6 | all-reduce | flops 1 | bytes 8 | tf_op jit(solution)/shard_map/psum | solution.py:78
  101.6 13.5 %all-reduce.16.cloned.1.call-done = f32[2,2,256,128]{3,2,1,0:T(8,128)} async-done(((f32[2,2,256,128]{3,2,1,0:T(8,128)}), f32[2,2,256,128]{3,2,1,0:T(8,128)}) %all-reduce.16.cloned.1.call-update) | async-done | bytes 524304 | tf_op jit(solution)/shard_map/psum | solution.py:68
  116.9 10.6 %psum.61 = f32[]{:T(128)} all-reduce(f32[]{:T(128)} %multiply_reduce_fusion.1), channel_id=1, replica_groups=mesh['slab'=8,'coil'=4] {'slab'}, use_global_device_ids=true, to_apply=%region_8.9 | all-reduce | flops 1 | bytes 8 | tf_op jit(solution)/shard_map/psum | solution.py:72
  138.8 12.3 %psum.62 = f32[]{:T(128)} all-reduce(f32[]{:T(128)S(6)} %add.664), channel_id=1, replica_groups=mesh['slab'=8,'coil'=4] {'slab'}, use_global_device_ids=true, to_apply=%region_11.12 | all-reduce | flops 1 | bytes 8 | tf_op jit(solution)/shard_map/psum | solution.py:78
  151.2 11.2 %psum.63 = f32[]{:T(128)} all-reduce(f32[]{:T(128)} %psum.62), channel_id=1, replica_groups=mesh['slab'=8,'coil'=4] {'coil'}, use_global_device_ids=true, to_apply=%region_12.13 | all-reduce | flops 1 | bytes 8 | tf_op jit(solution)/shard_map/psum | solution.py:78
  180.6 3.7 convolution_bitcast_fusion.29
  184.2 3.6 convolution_bitcast_fusion.30
  191.5 3.7 convolution_bitcast_fusion.33
  195.1 3.7 convolution_bitcast_fusion.35
  198.8 5.2 %fusion.22 = f32[32,2,64,128]{3,0,2,1:T(8,128)S(1)} fusion(f32[3,32,2,64,128]{4,1,3,2,0:T(8,128)S(1)} %convolution_bitcast_fusion.27, f32[3,32,2,64,128]{4,1,3,2,0:T(8,128)S(1)} %convolution_bitcast_fusion.28, f32[3,32,2,64,128]{4,1,3,2,0:T(8,128)} %convolution_bitcast_fusion.29, f32[3,32,2,64,128]{4,1,3,2,0:T(8,128)} %convolution_bitcast_fusion.30, ...), kind=kLoop, calls=%fused_computation.139 | loop fusion | flops 4194304 | bytes 20971520 | tf_op jit(solution)/shard_map/add | solution.py:107
  204.0 5.2 %fusion.30 = f32[32,2,64,128]{3,0,2,1:T(8,128)S(1)} fusion(f32[3,32,2,64,128]{4,1,3,2,0:T(8,128)S(1)} %convolution_bitcast_fusion.27, f32[3,32,2,64,128]{4,1,3,2,0:T(8,128)S(1)} %convolution_bitcast_fusion.28, f32[3,32,2,64,128]{4,1,3,2,0:T(8,128)} %convolution_bitcast_fusion.29, f32[3,32,2,64,128]{4,1,3,2,0:T(8,128)} %convolution_bitcast_fusion.30, ...), kind=kLoop, calls=%fused_computation.155 | loop fusion | flops 4194304 | bytes 20971520 | tf_op jit(solution)/shard_map/add | solution.py:107
  209.9 5.4 %fusion.35 = bf16[32,2,64,128]{3,0,2,1:T(8,128)(2,1)S(1)} fusion(f32[3,32,2,64,128]{4,1,3,2,0:T(8,128)S(1)} %convolution_bitcast_fusion.27, f32[3,32,2,64,128]{4,1,3,2,0:T(8,128)S(1)} %convolution_bitcast_fusion.28, f32[3,32,2,64,128]{4,1,3,2,0:T(8,128)} %convolution_bitcast_fusion.29, f32[3,32,2,64,128]{4,1,3,2,0:T(8,128)} %convolution_bitcast_fusion.30, ...), kind=kLoop, calls=%fused_computation.169 | loop fusion | flops 6291456 | bytes 24084480 | tf_op jit(solution)/shard_map/convert_element_type | solution.py:139
  224.1 8.6 %collective-permute-done.4 = bf16[32,1,64,128]{3,0,2,1:T(8,128)(2,1)S(1)} collective-permute-done((bf16[32,1,64,128]{3,0,2,1:T(8,128)(2,1)S(1)}, bf16[32,1,64,128]{3,0,2,1:T(8,128)(2,1)S(1)}, u32[]{:S(2)}, u32[]{:S(2)}) %collective-permute-start.4) | collective-permute-done | bytes 524320 | tf_op jit(solution)/shard_map/ppermute | solution.py:20
  238.0 3.7 convolution_bitcast_fusion.25
  263.9 13.9 %fusion.15 = (f32[32,2,64,128]{3,0,2,1:T(8,128)}, f32[32,2,64,128]{3,0,2,1:T(8,128)}) fusion(f32[3,32,2,64,128]{4,1,3,2,0:T(8,128)} %convolution_bitcast_fusion.18, f32[3,32,2,64,128]{4,1,3,2,0:T(8,128)S(1)} %convolution_bitcast_fusion.19, f32[3,32,2,64,128]{4,1,3,2,0:T(8,128)} %convolution_bitcast_fusion.20, ...), kind=kLoop, calls=%fused_computation.116 | loop fusion | flops 8388608 | bytes 41943040 | tf_op jit(solution)/shard_map/add | solution.py:107
  280.1 6.6 %fusion.20 = bf16[32,2,64,128]{3,0,2,1:T(8,128)(2,1)S(1)} fusion(f32[3,32,2,64,128]{4,1,3,2,0:T(8,128)} %convolution_bitcast_fusion.18, f32[3,32,2,64,128]{4,1,3,2,0:T(8,128)S(1)} %convolution_bitcast_fusion.19, f32[3,32,2,64,128]{4,1,3,2,0:T(8,128)} %convolution_bitcast_fusion.20, f32[3,32,2,64,128]{4,1,3,2,0:T(8,128)} %convolution_bitcast_fusion.21, ...), kind=kLoop, calls=%fused_computation.129 | loop fusion | flops 6291456 | bytes 24084480 | tf_op jit(solution)/shard_map/convert_element_type | solution.py:141
  295.4 6.4 %collective-permute-done.8 = bf16[32,1,64,128]{3,0,2,1:T(8,128)(2,1)S(1)} collective-permute-done((bf16[32,1,64,128]{3,0,2,1:T(8,128)(2,1)S(1)}, bf16[32,1,64,128]{3,0,2,1:T(8,128)(2,1)S(1)}, u32[]{:S(2)}, u32[]{:S(2)}) %collective-permute-start.8) | collective-permute-done | bytes 524320 | tf_op jit(solution)/shard_map/ppermute | solution.py:20
  301.8 4.6 collective-permute-start.10
  308.7 3.7 convolution_bitcast_fusion.16
  334.5 13.9 %fusion.8 = (f32[32,2,64,128]{3,0,2,1:T(8,128)}, f32[32,2,64,128]{3,0,2,1:T(8,128)}) fusion(f32[3,32,2,64,128]{4,1,3,2,0:T(8,128)} %convolution_bitcast_fusion.9, f32[3,32,2,64,128]{4,1,3,2,0:T(8,128)S(1)} %convolution_bitcast_fusion.10, f32[3,32,2,64,128]{4,1,3,2,0:T(8,128)} %convolution_bitcast_fusion.11, ...), kind=kLoop, calls=%fused_computation.85 | loop fusion | flops 8388608 | bytes 41943040 | tf_op jit(solution)/shard_map/add | solution.py:107
  350.8 6.6 %fusion.13 = bf16[32,2,64,128]{3,0,2,1:T(8,128)(2,1)S(1)} fusion(f32[3,32,2,64,128]{4,1,3,2,0:T(8,128)} %convolution_bitcast_fusion.9, f32[3,32,2,64,128]{4,1,3,2,0:T(8,128)S(1)} %convolution_bitcast_fusion.10, f32[3,32,2,64,128]{4,1,3,2,0:T(8,128)} %convolution_bitcast_fusion.11, f32[3,32,2,64,128]{4,1,3,2,0:T(8,128)} %convolution_bitcast_fusion.12, ...), kind=kLoop, calls=%fused_computation.98 | loop fusion | flops 6291456 | bytes 24084480 | tf_op jit(solution)/shard_map/convert_element_type | solution.py:141
  366.1 5.2 %collective-permute-done.12 = bf16[32,1,64,128]{3,0,2,1:T(8,128)(2,1)S(1)} collective-permute-done((bf16[32,1,64,128]{3,0,2,1:T(8,128)(2,1)S(1)}, bf16[32,1,64,128]{3,0,2,1:T(8,128)(2,1)S(1)}, u32[]{:S(2)}, u32[]{:S(2)}) %collective-permute-start.12) | collective-permute-done | bytes 524320 | tf_op jit(solution)/shard_map/ppermute | solution.py:20
  371.2 4.3 collective-permute-start.14
  377.8 3.7 convolution_bitcast_fusion.7
  403.6 13.9 %fusion.1 = (f32[32,2,64,128]{3,0,2,1:T(8,128)}, f32[32,2,64,128]{3,0,2,1:T(8,128)}) fusion(f32[3,32,2,64,128]{4,1,3,2,0:T(8,128)} %convolution_bitcast_fusion, f32[3,32,2,64,128]{4,1,3,2,0:T(8,128)S(1)} %convolution_bitcast_fusion.1, f32[3,32,2,64,128]{4,1,3,2,0:T(8,128)} %convolution_bitcast_fusion.2, f32[3,32,2,64,128]{4,1,3,2,0:T(8,128)} %convolution_bitcast_fusion.3, ...), kind=kLoop, calls=%fused_computation.54 | loop fusion | flops 8388608 | bytes 41943040 | tf_op jit(solution)/shard_map/add | solution.py:107
  419.9 6.6 %fusion.6 = bf16[32,2,64,128]{3,0,2,1:T(8,128)(2,1)S(1)} fusion(f32[3,32,2,64,128]{4,1,3,2,0:T(8,128)} %convolution_bitcast_fusion, f32[3,32,2,64,128]{4,1,3,2,0:T(8,128)S(1)} %convolution_bitcast_fusion.1, f32[3,32,2,64,128]{4,1,3,2,0:T(8,128)} %convolution_bitcast_fusion.2, f32[3,32,2,64,128]{4,1,3,2,0:T(8,128)} %convolution_bitcast_fusion.3, ...), kind=kLoop, calls=%fused_computation.67 | loop fusion | flops 6291456 | bytes 24084480 | tf_op jit(solution)/shard_map/convert_element_type | solution.py:141
  431.3 3.8 collective-permute-done.17
  435.2 4.7 %collective-permute-done.16 = bf16[32,1,64,128]{3,0,2,1:T(8,128)(2,1)S(1)} collective-permute-done((bf16[32,1,64,128]{3,0,2,1:T(8,128)(2,1)S(1)}, bf16[32,1,64,128]{3,0,2,1:T(8,128)(2,1)S(1)}, u32[]{:S(2)}, u32[]{:S(2)}) %collective-permute-start.16) | collective-permute-done | bytes 524320 | tf_op jit(solution)/shard_map/ppermute | solution.py:20
  439.9 4.5 collective-permute-start.18
  (162 shorter events, 181.9 us)
Async XLA Ops:
  7.2 53.9 %all-reduce.14.cloned.1.call-start = ((), (), s32[]{:S(2)}) async-start(), calls=%async_computation | async-start | bytes 1048576 | tf_op jit(solution)/shard_map/psum | solution.py:68
  13.9 2.4 copy-start.3
  16.3 1.0 copy-start.6
  17.3 97.8 %all-reduce.16.cloned.1.call-start = ((), (), s32[]{:S(2)}) async-start(), calls=%async_computation.1 | async-start | bytes 1048576 | tf_op jit(solution)/shard_map/psum | solution.py:68
  135.6 33.1 %copy-start.7 = (bf16[32,2,3,3,3]{0,1,4,3,2:T(2,128)(2,1)S(1)}, bf16[32,2,3,3,3]{0,1,4,3,2:T(2,128)(2,1)}, u32[]{:S(2)}) copy-start(bf16[32,2,3,3,3]{0,1,4,3,2:T(2,128)(2,1)} %param.11) | copy-start | bytes 10372
  164.4 5.4 %collective-permute-start.1 = (bf16[2,1,64,128]{3,2,1,0:T(8,128)(2,1)S(1)}, bf16[2,1,64,128]{3,2,1,0:T(8,128)(2,1)S(1)}, u32[]{:S(2)}, u32[]{:S(2)}) collective-permute-start(bf16[2,1,64,128]{3,2,1,0:T(8,128)(2,1)S(1)} %get-tuple-element.78), channel_id=1, source_target_pairs={{4,0},{8,4},{12,8},{16,12},{20,16},{24,20},{28,24},{5,1},{9,5},{13... | collective-permute-start | bytes 98312 | tf_op jit(solution)/shard_map/ppermute | solution.py:22
  166.3 6.0 %collective-permute-start = (bf16[2,1,64,128]{3,2,1,0:T(8,128)(2,1)S(1)}, bf16[2,1,64,128]{3,2,1,0:T(8,128)(2,1)S(1)}, u32[]{:S(2)}, u32[]{:S(2)}) collective-permute-start(bf16[2,1,64,128]{3,2,1,0:T(8,128)(2,1)S(1)} %get-tuple-element.77), channel_id=1, source_target_pairs={{0,4},{4,8},{8,12},{12,16},{16,20},{20,24},{24,28},{1,5},{5,9},{9,... | collective-permute-start | bytes 98312 | tf_op jit(solution)/shard_map/ppermute | solution.py:20
  172.3 5.2 %collective-permute-start.2 = (bf16[2,4,1,128]{3,2,1,0:T(2,128)(2,1)S(1)}, bf16[2,4,1,128]{3,2,1,0:T(2,128)(2,1)S(1)}, u32[]{:S(2)}, u32[]{:S(2)}) collective-permute-start(bf16[2,4,1,128]{3,2,1,0:T(2,128)(2,1)S(1)} %get-tuple-element.73), channel_id=1, source_target_pairs={{0,1},{1,2},{2,3},{4,5},{5,6},{6,7},{8,9},{9,10},{10,11},{12,13},{... | collective-permute-start | bytes 6152 | tf_op jit(solution)/shard_map/ppermute | solution.py:20
  173.9 5.5 %collective-permute-start.3 = (bf16[2,4,1,128]{3,2,1,0:T(2,128)(2,1)S(1)}, bf16[2,4,1,128]{3,2,1,0:T(2,128)(2,1)S(1)}, u32[]{:S(2)}, u32[]{:S(2)}) collective-permute-start(bf16[2,4,1,128]{3,2,1,0:T(2,128)(2,1)S(1)} %get-tuple-element.74), channel_id=1, source_target_pairs={{1,0},{2,1},{3,2},{5,4},{6,5},{7,6},{9,8},{10,9},{11,10},{13,12},{... | collective-permute-start | bytes 6152 | tf_op jit(solution)/shard_map/ppermute | solution.py:22
  215.3 4.6 copy-start.4
  215.4 8.7 %collective-permute-start.5 = (bf16[32,1,64,128]{3,0,2,1:T(8,128)(2,1)S(1)}, bf16[32,1,64,128]{3,0,2,1:T(8,128)(2,1)S(1)}, u32[]{:S(2)}, u32[]{:S(2)}) collective-permute-start(bf16[32,1,64,128]{3,0,2,1:T(8,128)(2,1)S(1)} %get-tuple-element.45), channel_id=1, source_target_pairs={{4,0},{8,4},{12,8},{16,12},{20,16},{24,20},{28,24},{5,1},{9,5},{13... | collective-permute-start | bytes 1572872 | tf_op jit(solution)/shard_map/ppermute | solution.py:22
  217.4 15.3 %collective-permute-start.4 = (bf16[32,1,64,128]{3,0,2,1:T(8,128)(2,1)S(1)}, bf16[32,1,64,128]{3,0,2,1:T(8,128)(2,1)S(1)}, u32[]{:S(2)}, u32[]{:S(2)}) collective-permute-start(bf16[32,1,64,128]{3,0,2,1:T(8,128)(2,1)S(1)} %get-tuple-element.44), channel_id=1, source_target_pairs={{0,4},{4,8},{8,12},{12,16},{16,20},{20,24},{24,28},{1,5},{5,9},{9,... | collective-permute-start | bytes 1572872 | tf_op jit(solution)/shard_map/ppermute | solution.py:20
  232.7 8.9 %collective-permute-start.6 = (bf16[32,4,1,128]{3,0,2,1:T(8,128)(2,1)S(1)}, bf16[32,4,1,128]{3,0,2,1:T(8,128)(2,1)S(1)}, u32[]{:S(2)}, u32[]{:S(2)}) collective-permute-start(bf16[32,4,1,128]{3,0,2,1:T(8,128)(2,1)S(1)} %get-tuple-element.32), channel_id=1, source_target_pairs={{0,1},{1,2},{2,3},{4,5},{5,6},{6,7},{8,9},{9,10},{10,11},{12,13},{... | collective-permute-start | bytes 98312 | tf_op jit(solution)/shard_map/ppermute | solution.py:20
  235.7 5.9 %collective-permute-start.7 = (bf16[32,4,1,128]{3,0,2,1:T(8,128)(2,1)S(1)}, bf16[32,4,1,128]{3,0,2,1:T(8,128)(2,1)S(1)}, u32[]{:S(2)}, u32[]{:S(2)}) collective-permute-start(bf16[32,4,1,128]{3,0,2,1:T(8,128)(2,1)S(1)} %get-tuple-element.33), channel_id=1, source_target_pairs={{1,0},{2,1},{3,2},{5,4},{6,5},{7,6},{9,8},{10,9},{11,10},{13,12},{... | collective-permute-start | bytes 98312 | tf_op jit(solution)/shard_map/ppermute | solution.py:22
  277.7 2.4 copy-start
  286.8 8.6 %collective-permute-start.9 = (bf16[32,1,64,128]{3,0,2,1:T(8,128)(2,1)S(1)}, bf16[32,1,64,128]{3,0,2,1:T(8,128)(2,1)S(1)}, u32[]{:S(2)}, u32[]{:S(2)}) collective-permute-start(bf16[32,1,64,128]{3,0,2,1:T(8,128)(2,1)S(1)} %get-tuple-element.43), channel_id=1, source_target_pairs={{4,0},{8,4},{12,8},{16,12},{20,16},{24,20},{28,24},{5,1},{9,5},{13... | collective-permute-start | bytes 1572872 | tf_op jit(solution)/shard_map/ppermute | solution.py:22
  288.7 13.1 %collective-permute-start.8 = (bf16[32,1,64,128]{3,0,2,1:T(8,128)(2,1)S(1)}, bf16[32,1,64,128]{3,0,2,1:T(8,128)(2,1)S(1)}, u32[]{:S(2)}, u32[]{:S(2)}) collective-permute-start(bf16[32,1,64,128]{3,0,2,1:T(8,128)(2,1)S(1)} %get-tuple-element.42), channel_id=1, source_target_pairs={{0,4},{4,8},{8,12},{12,16},{16,20},{20,24},{24,28},{1,5},{5,9},{9,... | collective-permute-start | bytes 1572872 | tf_op jit(solution)/shard_map/ppermute | solution.py:20
  301.8 10.5 %collective-permute-start.10 = (bf16[32,4,1,128]{3,0,2,1:T(8,128)(2,1)S(1)}, bf16[32,4,1,128]{3,0,2,1:T(8,128)(2,1)S(1)}, u32[]{:S(2)}, u32[]{:S(2)}) collective-permute-start(bf16[32,4,1,128]{3,0,2,1:T(8,128)(2,1)S(1)} %get-tuple-element.28), channel_id=1, source_target_pairs={{0,1},{1,2},{2,3},{4,5},{5,6},{6,7},{8,9},{9,10},{10,11},{12,13},{... | collective-permute-start | bytes 98312 | tf_op jit(solution)/shard_map/ppermute | solution.py:20
  306.4 5.9 %collective-permute-start.11 = (bf16[32,4,1,128]{3,0,2,1:T(8,128)(2,1)S(1)}, bf16[32,4,1,128]{3,0,2,1:T(8,128)(2,1)S(1)}, u32[]{:S(2)}, u32[]{:S(2)}) collective-permute-start(bf16[32,4,1,128]{3,0,2,1:T(8,128)(2,1)S(1)} %get-tuple-element.29), channel_id=1, source_target_pairs={{1,0},{2,1},{3,2},{5,4},{6,5},{7,6},{9,8},{10,9},{11,10},{13,12},{... | collective-permute-start | bytes 98312 | tf_op jit(solution)/shard_map/ppermute | solution.py:22
  348.4 2.4 copy-start.1
  357.4 8.6 %collective-permute-start.13 = (bf16[32,1,64,128]{3,0,2,1:T(8,128)(2,1)S(1)}, bf16[32,1,64,128]{3,0,2,1:T(8,128)(2,1)S(1)}, u32[]{:S(2)}, u32[]{:S(2)}) collective-permute-start(bf16[32,1,64,128]{3,0,2,1:T(8,128)(2,1)S(1)} %get-tuple-element.41), channel_id=1, source_target_pairs={{4,0},{8,4},{12,8},{16,12},{20,16},{24,20},{28,24},{5,1},{9,5},{13... | collective-permute-start | bytes 1572872 | tf_op jit(solution)/shard_map/ppermute | solution.py:22
  359.4 11.8 %collective-permute-start.12 = (bf16[32,1,64,128]{3,0,2,1:T(8,128)(2,1)S(1)}, bf16[32,1,64,128]{3,0,2,1:T(8,128)(2,1)S(1)}, u32[]{:S(2)}, u32[]{:S(2)}) collective-permute-start(bf16[32,1,64,128]{3,0,2,1:T(8,128)(2,1)S(1)} %get-tuple-element.40), channel_id=1, source_target_pairs={{0,4},{4,8},{8,12},{12,16},{16,20},{20,24},{24,28},{1,5},{5,9},{9,... | collective-permute-start | bytes 1572872 | tf_op jit(solution)/shard_map/ppermute | solution.py:20
  371.2 10.2 %collective-permute-start.14 = (bf16[32,4,1,128]{3,0,2,1:T(8,128)(2,1)S(1)}, bf16[32,4,1,128]{3,0,2,1:T(8,128)(2,1)S(1)}, u32[]{:S(2)}, u32[]{:S(2)}) collective-permute-start(bf16[32,4,1,128]{3,0,2,1:T(8,128)(2,1)S(1)} %get-tuple-element.24), channel_id=1, source_target_pairs={{0,1},{1,2},{2,3},{4,5},{5,6},{6,7},{8,9},{9,10},{10,11},{12,13},{... | collective-permute-start | bytes 98312 | tf_op jit(solution)/shard_map/ppermute | solution.py:20
  375.5 5.9 %collective-permute-start.15 = (bf16[32,4,1,128]{3,0,2,1:T(8,128)(2,1)S(1)}, bf16[32,4,1,128]{3,0,2,1:T(8,128)(2,1)S(1)}, u32[]{:S(2)}, u32[]{:S(2)}) collective-permute-start(bf16[32,4,1,128]{3,0,2,1:T(8,128)(2,1)S(1)} %get-tuple-element.25), channel_id=1, source_target_pairs={{1,0},{2,1},{3,2},{5,4},{6,5},{7,6},{9,8},{10,9},{11,10},{13,12},{... | collective-permute-start | bytes 98312 | tf_op jit(solution)/shard_map/ppermute | solution.py:22
  417.5 2.4 copy-start.2
  426.5 4.5 copy-start.8
  426.6 8.6 %collective-permute-start.17 = (bf16[32,1,64,128]{3,0,2,1:T(8,128)(2,1)S(1)}, bf16[32,1,64,128]{3,0,2,1:T(8,128)(2,1)S(1)}, u32[]{:S(2)}, u32[]{:S(2)}) collective-permute-start(bf16[32,1,64,128]{3,0,2,1:T(8,128)(2,1)S(1)} %get-tuple-element.39), channel_id=1, source_target_pairs={{4,0},{8,4},{12,8},{16,12},{20,16},{24,20},{28,24},{5,1},{9,5},{13... | collective-permute-start | bytes 1572872 | tf_op jit(solution)/shard_map/ppermute | solution.py:22
  428.5 11.4 %collective-permute-start.16 = (bf16[32,1,64,128]{3,0,2,1:T(8,128)(2,1)S(1)}, bf16[32,1,64,128]{3,0,2,1:T(8,128)(2,1)S(1)}, u32[]{:S(2)}, u32[]{:S(2)}) collective-permute-start(bf16[32,1,64,128]{3,0,2,1:T(8,128)(2,1)S(1)} %get-tuple-element.38), channel_id=1, source_target_pairs={{0,4},{4,8},{8,12},{12,16},{16,20},{20,24},{24,28},{1,5},{5,9},{9,... | collective-permute-start | bytes 1572872 | tf_op jit(solution)/shard_map/ppermute | solution.py:20
  439.9 6.8 %collective-permute-start.18 = (bf16[32,4,1,128]{3,0,2,1:T(8,128)(2,1)S(1)}, bf16[32,4,1,128]{3,0,2,1:T(8,128)(2,1)S(1)}, u32[]{:S(2)}, u32[]{:S(2)}) collective-permute-start(bf16[32,4,1,128]{3,0,2,1:T(8,128)(2,1)S(1)} %get-tuple-element.20), channel_id=1, source_target_pairs={{0,1},{1,2},{2,3},{4,5},{5,6},{6,7},{8,9},{9,10},{10,11},{12,13},{... | collective-permute-start | bytes 98312 | tf_op jit(solution)/shard_map/ppermute | solution.py:20
  444.5 5.8 %collective-permute-start.19 = (bf16[32,4,1,128]{3,0,2,1:T(8,128)(2,1)S(1)}, bf16[32,4,1,128]{3,0,2,1:T(8,128)(2,1)S(1)}, u32[]{:S(2)}, u32[]{:S(2)}) collective-permute-start(bf16[32,4,1,128]{3,0,2,1:T(8,128)(2,1)S(1)} %get-tuple-element.21), channel_id=1, source_target_pairs={{1,0},{2,1},{3,2},{5,4},{6,5},{7,6},{9,8},{10,9},{11,10},{13,12},{... | collective-permute-start | bytes 98312 | tf_op jit(solution)/shard_map/ppermute | solution.py:22
  453.1 0.9 copy-start.5
Sparse Core Ops, SparseCore 0:
  17.4 43.5 all-reduce.13
  76.5 38.5 all-reduce.15
